TPU v7x, 512 devices: a whole 4x8x8 slice. The times are simulated.
512 devices in a mesh: req: 128 (over z, x_hi, y), tensor: 4 (over x_lo, core).
Axes of the slice: x: 4 (x_hi: 2, x_lo: 2; x = x_hi * 2 + x_lo), y: 8, z: 8, core: 2. Of those that a mesh axis runs over, the one named last changes fastest.
Arguments:
- tokens: bfloat16 [32768, 2048], P('req'), may hold values from -6 to 6
- segment_ids: int32 [128, 256], P('req'), may hold values from 0 to 7, never falling along the last dimension, each value on 1 to 128 neighbouring positions
- padding: int32 [32768], P('req'), may hold values 0 or 1
- attn_experts: int32 [32768, 2], P('req'), may hold values from 0 to 3, all different within a row
- gain: float32 [2048], replicated, may hold values from 0.1 to 1.9
- w_router: float32 [2048, 4], replicated, may hold values from -0.125 to 0.125
- w_query: bfloat16 [2048, 4096], P('req', 'tensor'), may hold values from -1 to 1
- w_kv: bfloat16 [2048, 2048], P('req', 'tensor'), may hold values from -1 to 1
- w_out: bfloat16 [4096, 2048], P('tensor', 'req'), may hold values from -0.1875 to 0.1875
- page_shift: int32 [16], replicated, may hold values from 0 to 15, as said below
Outputs:
- attended: bfloat16 [32768, 2048], P('req', 'tensor')
- kv_cache: bfloat16 [2048, 16, 2048], P('req', None, 'tensor')
Inputs may be any that keep to these rules, and one draw needn't show every extreme that they name: `segment_ids`: segment ids never fall along a batch; each of the 8 prompts holds at least one token and at most 128. `attn_experts`: the two experts of a token differ. Block j of every batch goes to the owner page_shift[j] places further along req, cyclically, into that owner's block j.
All inputs are finite; a program needn't handle non-finite values. No bound on the sum of `padding` on one device may be relied on, other than what follows from the above.
Results may differ from a plain program's by a relative error of at most 0.013.
Values may be sent and summed in bfloat16 or wider, within the bound.
A program may use at most 64 MiB of HBM per device.

v0:
```python
import jax
import jax.numpy as jnp
from jax import lax
from jax.sharding import PartitionSpec as P

HD = 128
EXPERTS = 4
BITS = 4


def from_behind(value, axis, steps):
    count = lax.axis_size(axis)
    pairs = [(source, (source + steps) % count) for source in range(count)]
    return lax.ppermute(value, axis, pairs)


def rotate(values, position):
    half_size = values.shape[-1] // 2
    freqs = 10000.0 ** (-jnp.arange(half_size, dtype=jnp.float32) / half_size)
    angles = position.astype(jnp.float32)[:, None] * freqs[None, :]
    angles = angles.reshape((values.shape[0],) + (1,) * (values.ndim - 2) + (half_size,))
    cosine = jnp.cos(angles)
    sine = jnp.sin(angles)
    first = values[..., :half_size]
    second = values[..., half_size:]
    return jnp.concatenate(
        [first * cosine - second * sine, second * cosine + first * sine], axis=-1
    )


def allowed_mask(seg_row, pad_row, query_index, key_index):
    allowed = (seg_row[query_index][:, None] == seg_row[key_index][None, :]) & (
        key_index[None, :] <= query_index[:, None]
    )
    return allowed & (
        (pad_row[key_index][None, :] == 1) | (key_index[None, :] == query_index[:, None])
    )


def attend_dense(queries, keys, values, seg_row, pad_row):
    count = queries.shape[0]
    index = jnp.arange(count, dtype=jnp.int32)
    allowed = allowed_mask(seg_row, pad_row, index, index)
    scores = jnp.einsum(
        "tshd,uhd->shtu", queries, keys, preferred_element_type=jnp.float32
    ) / jnp.sqrt(jnp.float32(queries.shape[-1]))
    masked = jnp.where(allowed[None, None], scores, -1e30)
    peak = jnp.max(masked, axis=3, keepdims=True)
    weights = jnp.where(allowed[None, None], jnp.exp(masked - peak), 0.0)
    total = jnp.sum(weights, axis=3)
    summed = jnp.einsum(
        "shtu,uhd->tshd", weights.astype(jnp.bfloat16), values, preferred_element_type=jnp.float32
    )
    return summed / jnp.transpose(total, (2, 0, 1))[:, :, :, None]


def on_device(
    tokens, segment_ids, padding, attn_experts, gain, w_router, w_query, w_kv, w_out, page_shift
):
    count = tokens.shape[0]
    seg_row = segment_ids[0]
    starts = jnp.sum((seg_row[None, :] < seg_row[:, None]).astype(jnp.int32), axis=1)
    position = jnp.arange(count, dtype=jnp.int32) - starts
    x_float = tokens.astype(jnp.float32)
    normed = (
        x_float
        * lax.rsqrt(jnp.mean(x_float * x_float, axis=1, keepdims=True) + 1e-06)
        * gain[None, :]
    ).astype(jnp.bfloat16)
    pad_float = padding.astype(jnp.float32)
    local_heads = w_kv.shape[1] // (2 * HD)

    def add_rows(piece):
        return jnp.dot(normed, piece, preferred_element_type=jnp.float32)

    keyval = add_rows(lax.all_gather(w_kv, "req", axis=0, tiled=True))
    query_all = add_rows(lax.all_gather(w_query, "req", axis=0, tiled=True))
    keyval = keyval.reshape(count, local_heads, 2, HD)
    keys_rot = rotate(keyval[:, :, 0, :], position)
    keyval = (
        jnp.stack([keys_rot, keyval[:, :, 1, :]], axis=2) * pad_float[:, None, None, None]
    ).astype(jnp.bfloat16)
    logits = jnp.dot(normed.astype(jnp.float32), w_router, preferred_element_type=jnp.float32)
    selector = (
        attn_experts[:, :, None] == jnp.arange(EXPERTS, dtype=jnp.int32)[None, None, :]
    ).astype(jnp.float32)
    gates = jnp.einsum("tse,te->ts", selector, jax.nn.sigmoid(logits))
    query_all = rotate(query_all.reshape(count, local_heads, EXPERTS, HD), position)
    queries = jnp.einsum("thed,tse->tshd", query_all, selector).astype(jnp.bfloat16)
    keys_b = keyval[:, :, 0, :]
    values_b = keyval[:, :, 1, :]
    heads_out = attend_dense(queries, keys_b, values_b, seg_row, padding)
    mixed = (
        jnp.einsum("tshd,tse->thed", heads_out * gates[:, :, None, None], selector)
        * pad_float[:, None, None, None]
    )
    mixed = mixed.reshape(count, local_heads * EXPERTS * HD).astype(jnp.bfloat16)
    partial_out = jnp.dot(
        mixed, lax.all_gather(w_out, "req", axis=1, tiled=True), preferred_element_type=jnp.float32
    )
    attended = lax.psum_scatter(
        partial_out.astype(jnp.bfloat16), "tensor", scatter_dimension=1, tiled=True
    )
    page_count = page_shift.shape[0]
    page_size = count // page_count
    pages = keyval.reshape(page_count, page_size, local_heads * 2 * HD)
    for level in range(BITS):
        moved = from_behind(pages, "req", 2**level)
        taken = page_shift // 2**level % 2 == 1
        pages = jnp.where(taken[:, None, None], moved, pages)
    return (attended, pages)


def solution(mesh):
    placed = (
        P("req", None),
        P("req", None),
        P("req"),
        P("req", None),
        P(),
        P(),
        P("req", "tensor"),
        P("req", "tensor"),
        P("tensor", "req"),
        P(),
    )
    return jax.shard_map(
        on_device,
        mesh=mesh,
        in_specs=placed,
        out_specs=(P("req", "tensor"), P("req", None, "tensor")),
        check_vma=False,
    )
```

profile of v0, /device:TPU:2, one launch (start us, length us, event | category | flops | bytes accessed | tf_op | source)
XLA Modules:
  0.0 492.8 jit_solution(6888651575733452197)
XLA Ops:
  7.2 0.7 all-gather.4.cloned.1.call-update
  8.0 0.7 all-gather.6.cloned.1.call-update
  8.7 0.7 all-gather.8.cloned.1.call-update
  9.5 0.7 convert_element_type.50
  10.2 0.8 copy.27
  11.1 2.0 gather_fusion.1
  13.1 2.0 gather_fusion
  15.1 0.3 fusion.1
  15.4 0.5 fusion.15
  15.8 0.2 copy.48
  16.0 0.9 fusion.22
  17.0 0.2 convert_reduce_fusion
  17.2 0.1 fusion.25
  17.3 0.5 multiply_cosine_fusion
  17.9 127.1 %all-gather.4.cloned.1.call-done = bf16[2048,512]{1,0:T(8,128)(2,1)} async-done(((bf16[16,512]{1,0:T(8,128)(2,1)}), bf16[2048,512]{1,0:T(8,128)(2,1)}) %all-gather.4.cloned.1.call-update) | async-done | bytes 2097168 | tf_op jit(solution)/shard_map/all_gather | solution.py:76
  145.0 2.3 fusion.46
  147.3 0.3 reshape.219
  147.6 0.4 fusion.48
  148.1 0.2 multiply_subtract_fusion.1
  148.3 0.1 maximum_bitcast_fusion
  148.4 0.1 pad_maximum_fusion
  148.5 0.4 copy.34
  149.0 0.4 stack.10
  149.4 133.6 %all-gather.6.cloned.1.call-done = bf16[2048,1024]{1,0:T(8,128)(2,1)} async-done(((bf16[16,1024]{1,0:T(8,128)(2,1)}), bf16[2048,1024]{1,0:T(8,128)(2,1)}) %all-gather.6.cloned.1.call-update) | async-done | bytes 4194320 | tf_op jit(solution)/shard_map/all_gather | solution.py:77
  283.0 3.5 fusion.44
  286.5 0.5 reshape.220
  287.0 0.8 multiply_subtract_fusion
  287.8 1.2 convolution_convert_fusion.1
  289.0 0.6 fusion.49
  289.6 0.3 fusion.8
  289.9 0.4 fusion.12
  290.4 0.2 copy.33
  290.5 1.4 fusion.10
  292.0 0.4 convert_element_type.56
  292.3 128.7 %all-gather.8.cloned.1.call-done = bf16[1024,2048]{0,1:T(8,128)(2,1)} async-done(((bf16[1024,16]{0,1:T(8,128)(2,1)}), bf16[1024,2048]{0,1:T(8,128)(2,1)}) %all-gather.8.cloned.1.call-update) | async-done | bytes 4194320 | tf_op jit(solution)/shard_map/all_gather | solution.py:99
  421.0 4.4 convolution_convert_fusion
  425.5 0.1 multiply_convert_fusion
  425.6 2.9 collective-permute-start
  428.6 11.1 %collective-permute-done = bf16[16,16,512]{2,1,0:T(8,128)(2,1)S(1)} collective-permute-done((bf16[16,16,512]{2,1,0:T(8,128)(2,1)S(1)}, bf16[16,16,512]{2,1,0:T(8,128)(2,1)S(1)}, u32[]{:S(2)}, u32[]{:S(2)}) %collective-permute-start) | collective-permute-done | bytes 262176 | tf_op jit(solution)/shard_map/ppermute | solution.py:14
  439.7 0.1 broadcast_select_fusion
  439.9 1.9 collective-permute-start.1
  441.8 13.0 %collective-permute-done.1 = bf16[16,16,512]{2,1,0:T(8,128)(2,1)S(1)} collective-permute-done((bf16[16,16,512]{2,1,0:T(8,128)(2,1)S(1)}, bf16[16,16,512]{2,1,0:T(8,128)(2,1)S(1)}, u32[]{:S(2)}, u32[]{:S(2)}) %collective-permute-start.1) | collective-permute-done | bytes 262176 | tf_op jit(solution)/shard_map/ppermute | solution.py:14
  454.7 0.1 broadcast_select_fusion.1
  454.8 1.9 collective-permute-start.2
  456.8 16.3 %collective-permute-done.2 = bf16[16,16,512]{2,1,0:T(8,128)(2,1)S(1)} collective-permute-done((bf16[16,16,512]{2,1,0:T(8,128)(2,1)S(1)}, bf16[16,16,512]{2,1,0:T(8,128)(2,1)S(1)}, u32[]{:S(2)}, u32[]{:S(2)}) %collective-permute-start.2) | collective-permute-done | bytes 262176 | tf_op jit(solution)/shard_map/ppermute | solution.py:14
  473.2 1.9 collective-permute-start.3
  475.1 10.4 %collective-permute-done.3 = bf16[16,16,512]{2,1,0:T(8,128)(2,1)S(1)} collective-permute-done((bf16[16,16,512]{2,1,0:T(8,128)(2,1)S(1)}, bf16[16,16,512]{2,1,0:T(8,128)(2,1)S(1)}, u32[]{:S(2)}, u32[]{:S(2)}) %collective-permute-start.3) | collective-permute-done | bytes 262176 | tf_op jit(solution)/shard_map/ppermute | solution.py:14
  485.5 0.8 broadcast_select_fusion.3
  (28 shorter events, 0.5 us)
Async XLA Ops:
  7.2 8.2 %copy-start = (f32[2048,4]{0,1:T(4,128)S(1)}, f32[2048,4]{0,1:T(4,128)}, u32[]{:S(2)}) copy-start(f32[2048,4]{0,1:T(4,128)} %param.15) | copy-start | bytes 98308
  7.2 7.9 %copy-start.2 = (bf16[256,2048]{1,0:T(8,128)(2,1)S(1)}, bf16[256,2048]{1,0:T(8,128)(2,1)}, u32[]{:S(2)}) copy-start(bf16[256,2048]{1,0:T(8,128)(2,1)} %param.10) | copy-start | bytes 3145732
  7.2 8.2 %copy-start.4 = (f32[2048]{0:T(1024)S(1)}, f32[2048]{0:T(1024)}, u32[]{:S(2)}) copy-start(f32[2048]{0:T(1024)} %param.14) | copy-start | bytes 24580
  7.2 137.8 %all-gather.4.cloned.1.call-start = ((), (), s32[]{:S(2)}) async-start(), calls=%async_computation.1 | async-start | bytes 2113536 | tf_op jit(solution)/shard_map/all_gather | solution.py:76
  7.9 275.1 %all-gather.6.cloned.1.call-start = ((), (), s32[]{:S(2)}) async-start(), calls=%async_computation.2 | async-start | bytes 4227072 | tf_op jit(solution)/shard_map/all_gather | solution.py:77
  8.7 412.3 %all-gather.8.cloned.1.call-start = ((), (), s32[]{:S(2)}) async-start(), calls=%async_computation.3 | async-start | bytes 4227072 | tf_op jit(solution)/shard_map/all_gather | solution.py:99
  9.4 476.9 %reduce-scatter.2.cloned.1.call-start = ((), (), s32[]{:S(2)}) async-start(), calls=%async_computation.4 | async-start | bytes 1310720 | tf_op jit(solution)/shard_map/reduce_scatter | solution.py:101
  15.0 1.9 copy-start.1
  292.3 136.2 %copy-start.3 = (s32[16]{0:T(128)S(1)}, s32[16]{0:T(128)}, u32[]{:S(2)}) copy-start(s32[16]{0:T(128)} %param.19) | copy-start | bytes 196
  425.6 14.1 %collective-permute-start = (bf16[16,16,512]{2,1,0:T(8,128)(2,1)S(1)}, bf16[16,16,512]{2,1,0:T(8,128)(2,1)S(1)}, u32[]{:S(2)}, u32[]{:S(2)}) collective-permute-start(bf16[16,16,512]{2,1,0:T(8,128)(2,1)S(1)} %multiply_convert_fusion), channel_id=1, source_target_pairs={{0,4},{4,8},{8,12},{12,16},{16,20},{20,24},{24,28},{28,32},{32,36}... | collective-permute-start | bytes 786440 | tf_op jit(solution)/shard_map/ppermute | solution.py:14
  439.9 14.9 %collective-permute-start.1 = (bf16[16,16,512]{2,1,0:T(8,128)(2,1)S(1)}, bf16[16,16,512]{2,1,0:T(8,128)(2,1)S(1)}, u32[]{:S(2)}, u32[]{:S(2)}) collective-permute-start(bf16[16,16,512]{2,1,0:T(8,128)(2,1)S(1)} %broadcast_select_fusion), channel_id=1, source_target_pairs={{0,8},{4,12},{8,16},{12,20},{16,24},{20,28},{24,32},{28,36},{32,40... | collective-permute-start | bytes 786440 | tf_op jit(solution)/shard_map/ppermute | solution.py:14
  454.8 18.2 %collective-permute-start.2 = (bf16[16,16,512]{2,1,0:T(8,128)(2,1)S(1)}, bf16[16,16,512]{2,1,0:T(8,128)(2,1)S(1)}, u32[]{:S(2)}, u32[]{:S(2)}) collective-permute-start(bf16[16,16,512]{2,1,0:T(8,128)(2,1)S(1)} %broadcast_select_fusion.1), channel_id=1, source_target_pairs={{0,16},{4,20},{8,24},{12,28},{16,32},{20,36},{24,40},{28,44},{32,4... | collective-permute-start | bytes 786440 | tf_op jit(solution)/shard_map/ppermute | solution.py:14
  473.2 12.3 %collective-permute-start.3 = (bf16[16,16,512]{2,1,0:T(8,128)(2,1)S(1)}, bf16[16,16,512]{2,1,0:T(8,128)(2,1)S(1)}, u32[]{:S(2)}, u32[]{:S(2)}) collective-permute-start(bf16[16,16,512]{2,1,0:T(8,128)(2,1)S(1)} %broadcast_select_fusion.2), channel_id=1, source_target_pairs={{0,32},{4,36},{8,40},{12,44},{16,48},{20,52},{24,56},{28,60},{32,6... | collective-permute-start | bytes 786440 | tf_op jit(solution)/shard_map/ppermute | solution.py:14
Sparse Core Ops, SparseCore 0:
  12.5 132.3 all-gather.3
  149.3 133.6 all-gather.5
  287.4 133.5 all-gather.7
  425.6 23.1 reduce-scatter.1
where the time goes:
time: 493 us
  waiting for transfers between devices  442 us (90%)
  matrix products  14.7 us (3%)
  between operations  14.1 us (3%)
  starting transfers between devices  8.84 us (2%)
  local copies, waits for them, and re-layouts  7.76 us (2%)
  other arithmetic  5.18 us (1%)
    all_gather x1, waiting for transfers between devices, on_device(): query_all = add_rows(lax.all_gather(w_query, 'req', axis=0, tiled=True))  134 us
    all_gather x1, waiting for transfers between devices, on_device(): lax.all_gather(w_out, 'req', axis=1, tiled=True)  129 us
    all_gather x1, waiting for transfers between devices, on_device(): keyval = add_rows(lax.all_gather(w_kv, 'req', axis=0, tiled=True))  127 us
    ppermute x4, waiting for transfers between devices, from_behind(): return lax.ppermute(value, axis, pairs)  50.8 us
  transfers between devices with their start and end apart: 8, of which 7 were waited for; matrix products, arithmetic and copies ran while one was open for 5% of the time, Pallas kernels for 0%

commit v1 on v0

--- a/solution.py
+++ b/solution.py
@@ -73,7 +73,11 @@
     def add_rows(piece):
         return jnp.dot(normed, piece, preferred_element_type=jnp.float32)
 
-    keyval = add_rows(lax.all_gather(w_kv, "req", axis=0, tiled=True))
+    keyval = add_rows(
+        jnp.concatenate(
+            lax.all_to_all(jnp.stack([w_kv] * lax.axis_size("req")), "req", 0, 0), axis=0
+        )
+    )
     query_all = add_rows(lax.all_gather(w_query, "req", axis=0, tiled=True))
     keyval = keyval.reshape(count, local_heads, 2, HD)
     keys_rot = rotate(keyval[:, :, 0, :], position)

time: 493 us -> 395 us (0.80)
  waiting for transfers between devices: 442 us -> 317 us
  starting transfers between devices: 8.84 us -> 28.5 us
  local copies, waits for them, and re-layouts: 7.76 us -> 14.5 us
    all_gather x1 -> x0, waiting for transfers between devices: 127 us -> none  [on_device(): keyval = add_rows(lax.all_gather(w_kv, 'req', axis=0, tiled=True))]
    all_to_all x0 -> x1, waiting for transfers between devices: none -> 43.5 us  [on_device(): lax.all_to_all(jnp.stack([w_kv] * lax.axis_size('req')), 'req', 0, 0)]
    all_gather x1, waiting for transfers between devices: 134 us -> 93.2 us  [on_device(): query_all = add_rows(lax.all_gather(w_query, 'req', axis=0, tiled=True))]
    all_to_all x0 -> x1, starting transfers between devices: none -> 19.5 us  [on_device(): lax.all_to_all(jnp.stack([w_kv] * lax.axis_size('req')), 'req', 0, 0)]
  transfers between devices with their start and end apart: 8 -> 8, of which waited for: 7 -> 7; matrix products, arithmetic and copies ran while one was open for 5% -> 8% of each run, Pallas kernels for 0% -> 0%
where the time goes in v1:
time: 395 us; the launch traced here: 394 us
  waiting for transfers between devices  317 us (80%)
  starting transfers between devices  28.5 us (7%)
  matrix products  14.9 us (4%)
  local copies, waits for them, and re-layouts  14.5 us (4%)
  between operations  14.1 us (4%)
  other arithmetic  5.48 us (1%)
    all_gather x1, waiting for transfers between devices, on_device(): lax.all_gather(w_out, 'req', axis=1, tiled=True)  128 us
    all_gather x1, waiting for transfers between devices, on_device(): query_all = add_rows(lax.all_gather(w_query, 'req', axis=0, tiled=True))  93.2 us
    ppermute x4, waiting for transfers between devices, from_behind(): return lax.ppermute(value, axis, pairs)  50.8 us
    all_to_all x1, waiting for transfers between devices, on_device(): lax.all_to_all(jnp.stack([w_kv] * lax.axis_size('req')), 'req', 0, 0)  43.5 us
    all_to_all x1, starting transfers between devices, on_device(): lax.all_to_all(jnp.stack([w_kv] * lax.axis_size('req')), 'req', 0, 0)  19.5 us
    ppermute x4, starting transfers between devices, from_behind(): return lax.ppermute(value, axis, pairs)  8.69 us
  transfers between devices with their start and end apart: 8, of which 7 were waited for; matrix products, arithmetic and copies ran while one was open for 8% of the time, Pallas kernels for 0%

profile of v1, /device:TPU:2, one launch (start us, length us, event | category | flops | bytes accessed | tf_op | source)
XLA Modules:
  0.0 394.4 jit_solution(324088097482953899)
XLA Ops:
  7.2 0.7 all-gather.3.cloned.1.call-update
  8.0 0.7 all-gather.5.cloned.1.call-update
  8.7 2.3 stack.8
  11.0 19.5 %all-to-all-start = ((bf16[128,16,512]{2,1,0:T(8,128)(2,1)}), bf16[128,16,512]{2,1,0:T(8,128)(2,1)S(1)}, u32[]{:S(2)}, u32[]{:S(2)}) async-start(bf16[128,16,512]{2,1,0:T(8,128)(2,1)} %stack.8), calls=%async_computation | async-start | bytes 4194304 | tf_op jit(solution)/shard_map/all_to_all | solution.py:78
  30.6 0.2 reduce-scatter.2.cloned.1.call-start
  30.9 1.9 gather_fusion.1
  32.9 1.9 gather_fusion
  34.8 0.2 convert_reduce_fusion
  35.0 0.3 multiply_cosine_fusion
  35.3 0.8 copy.39
  36.1 0.8 copy.40
  36.8 0.1 copy.36
  37.0 0.3 fusion.1
  37.3 0.5 fusion.15
  37.8 0.8 copy.59
  38.6 2.4 fusion.24
  41.0 1.0 copy.55
  41.9 0.1 fusion.27
  42.1 43.5 %all-to-all-done = bf16[128,16,512]{2,1,0:T(8,128)(2,1)S(1)} async-done(((bf16[128,16,512]{2,1,0:T(8,128)(2,1)}), bf16[128,16,512]{2,1,0:T(8,128)(2,1)S(1)}, u32[]{:S(2)}, u32[]{:S(2)}) %all-to-all-start) | async-done | bytes 2097184 | tf_op jit(solution)/shard_map/all_to_all | solution.py:78
  85.6 2.5 copy.37
  88.1 2.4 fusion.19
  90.7 0.3 copy.45
  91.0 0.4 stack.11
  91.4 93.2 %all-gather.3.cloned.1.call-done = bf16[2048,1024]{1,0:T(8,128)(2,1)} async-done(((bf16[16,1024]{1,0:T(8,128)(2,1)}), bf16[2048,1024]{1,0:T(8,128)(2,1)}) %all-gather.3.cloned.1.call-update) | async-done | bytes 4194320 | tf_op jit(solution)/shard_map/all_gather | solution.py:81
  184.7 3.5 fusion.46
  188.2 0.5 reshape.224
  188.7 0.4 copy-done.4
  189.1 0.8 multiply_subtract_fusion
  189.9 1.2 convolution_convert_fusion.1
  191.1 0.6 fusion.49
  191.8 0.4 fusion.8
  192.2 0.4 fusion.12
  192.6 0.2 copy.44
  192.8 1.4 fusion.10
  194.2 0.4 convert_element_type.56
  194.6 128.1 %all-gather.5.cloned.1.call-done = bf16[1024,2048]{0,1:T(8,128)(2,1)} async-done(((bf16[1024,16]{0,1:T(8,128)(2,1)}), bf16[1024,2048]{0,1:T(8,128)(2,1)}) %all-gather.5.cloned.1.call-update) | async-done | bytes 4194320 | tf_op jit(solution)/shard_map/all_gather | solution.py:103
  322.7 4.4 %convolution_convert_fusion = bf16[256,2048]{1,0:T(8,128)(2,1)} fusion(bf16[256,1024]{1,0:T(8,128)(2,1)S(1)} %convert_element_type.56, bf16[1024,2048]{0,1:T(8,128)(2,1)} %all-gather.5.cloned.1.call-done), kind=kOutput, calls=%fused_computation.5 | convolution fusion | flops 1074266112 | bytes 5767168 | tf_op jit(solution)/shard_map/dot_general | solution.py:102
  327.1 0.1 multiply_convert_fusion
  327.2 2.9 collective-permute-start
  330.2 11.1 %collective-permute-done = bf16[16,16,512]{2,1,0:T(8,128)(2,1)S(1)} collective-permute-done((bf16[16,16,512]{2,1,0:T(8,128)(2,1)S(1)}, bf16[16,16,512]{2,1,0:T(8,128)(2,1)S(1)}, u32[]{:S(2)}, u32[]{:S(2)}) %collective-permute-start) | collective-permute-done | bytes 262176 | tf_op jit(solution)/shard_map/ppermute | solution.py:14
  341.3 0.1 broadcast_select_fusion
  341.5 1.9 collective-permute-start.1
  343.4 13.0 %collective-permute-done.1 = bf16[16,16,512]{2,1,0:T(8,128)(2,1)S(1)} collective-permute-done((bf16[16,16,512]{2,1,0:T(8,128)(2,1)S(1)}, bf16[16,16,512]{2,1,0:T(8,128)(2,1)S(1)}, u32[]{:S(2)}, u32[]{:S(2)}) %collective-permute-start.1) | collective-permute-done | bytes 262176 | tf_op jit(solution)/shard_map/ppermute | solution.py:14
  356.5 1.9 collective-permute-start.2
  358.4 16.3 %collective-permute-done.2 = bf16[16,16,512]{2,1,0:T(8,128)(2,1)S(1)} collective-permute-done((bf16[16,16,512]{2,1,0:T(8,128)(2,1)S(1)}, bf16[16,16,512]{2,1,0:T(8,128)(2,1)S(1)}, u32[]{:S(2)}, u32[]{:S(2)}) %collective-permute-start.2) | collective-permute-done | bytes 262176 | tf_op jit(solution)/shard_map/ppermute | solution.py:14
  374.8 1.9 collective-permute-start.3
  376.7 10.4 %collective-permute-done.3 = bf16[16,16,512]{2,1,0:T(8,128)(2,1)S(1)} collective-permute-done((bf16[16,16,512]{2,1,0:T(8,128)(2,1)S(1)}, bf16[16,16,512]{2,1,0:T(8,128)(2,1)S(1)}, u32[]{:S(2)}, u32[]{:S(2)}) %collective-permute-start.3) | collective-permute-done | bytes 262176 | tf_op jit(solution)/shard_map/ppermute | solution.py:14
  387.1 0.8 broadcast_select_fusion.3
  (36 shorter events, 0.7 us)
Async XLA Ops:
  7.2 30.1 %copy-start = (f32[2048,4]{0,1:T(4,128)S(1)}, f32[2048,4]{0,1:T(4,128)}, u32[]{:S(2)}) copy-start(f32[2048,4]{0,1:T(4,128)} %param.15) | copy-start | bytes 98308
  7.2 177.5 %all-gather.3.cloned.1.call-start = ((), (), s32[]{:S(2)}) async-start(), calls=%async_computation.2 | async-start | bytes 4227072 | tf_op jit(solution)/shard_map/all_gather | solution.py:81
  7.9 314.7 %all-gather.5.cloned.1.call-start = ((), (), s32[]{:S(2)}) async-start(), calls=%async_computation.3 | async-start | bytes 4227072 | tf_op jit(solution)/shard_map/all_gather | solution.py:103
  11.0 19.8 %copy-start.2 = (s32[256]{0:T(256)S(1)}, s32[256]{0:T(256)}, u32[]{:S(2)}) copy-start(s32[256]{0:T(256)} %param.12) | copy-start | bytes 3076
  11.0 21.8 %copy-start.1 = (s32[1,256]{1,0:T(1,128)S(1)}, s32[1,256]{1,0:T(1,128)}, u32[]{:S(2)}) copy-start(s32[1,256]{1,0:T(1,128)} %param.11) | copy-start | bytes 3076
  11.0 74.6 %all-to-all-start = ((bf16[128,16,512]{2,1,0:T(8,128)(2,1)}), bf16[128,16,512]{2,1,0:T(8,128)(2,1)S(1)}, u32[]{:S(2)}, u32[]{:S(2)}) async-start(bf16[128,16,512]{2,1,0:T(8,128)(2,1)} %stack.8), calls=%async_computation | async-start | bytes 4194304 | tf_op jit(solution)/shard_map/all_to_all | solution.py:78
  30.5 6.3 %copy-start.6 = (s32[256,2]{0,1:T(2,128)S(1)}, s32[256,2]{0,1:T(2,128)}, u32[]{:S(2)}) copy-start(s32[256,2]{0,1:T(2,128)} %param.13) | copy-start | bytes 6148
  30.5 6.5 %copy-start.3 = (bf16[256,2048]{1,0:T(8,128)(2,1)S(1)}, bf16[256,2048]{1,0:T(8,128)(2,1)}, u32[]{:S(2)}) copy-start(bf16[256,2048]{1,0:T(8,128)(2,1)} %param.10) | copy-start | bytes 3145732
  30.5 6.8 %copy-start.8 = (f32[2048]{0:T(1024)S(1)}, f32[2048]{0:T(1024)}, u32[]{:S(2)}) copy-start(f32[2048]{0:T(1024)} %param.14) | copy-start | bytes 24580
  30.6 357.4 %reduce-scatter.2.cloned.1.call-start = ((), (), s32[]{:S(2)}) async-start(), calls=%async_computation.4 | async-start | bytes 1310720 | tf_op jit(solution)/shard_map/reduce_scatter | solution.py:105
  188.1 0.9 copy-start.4
  188.1 1.0 copy-start.5
  194.5 135.6 %copy-start.7 = (s32[16]{0:T(128)S(1)}, s32[16]{0:T(128)}, u32[]{:S(2)}) copy-start(s32[16]{0:T(128)} %param.19) | copy-start | bytes 196
  327.2 14.1 %collective-permute-start = (bf16[16,16,512]{2,1,0:T(8,128)(2,1)S(1)}, bf16[16,16,512]{2,1,0:T(8,128)(2,1)S(1)}, u32[]{:S(2)}, u32[]{:S(2)}) collective-permute-start(bf16[16,16,512]{2,1,0:T(8,128)(2,1)S(1)} %multiply_convert_fusion), channel_id=1, source_target_pairs={{0,4},{4,8},{8,12},{12,16},{16,20},{20,24},{24,28},{28,32},{32,36}... | collective-permute-start | bytes 786440 | tf_op jit(solution)/shard_map/ppermute | solution.py:14
  341.5 14.9 %collective-permute-start.1 = (bf16[16,16,512]{2,1,0:T(8,128)(2,1)S(1)}, bf16[16,16,512]{2,1,0:T(8,128)(2,1)S(1)}, u32[]{:S(2)}, u32[]{:S(2)}) collective-permute-start(bf16[16,16,512]{2,1,0:T(8,128)(2,1)S(1)} %broadcast_select_fusion), channel_id=1, source_target_pairs={{0,8},{4,12},{8,16},{12,20},{16,24},{20,28},{24,32},{28,36},{32,40... | collective-permute-start | bytes 786440 | tf_op jit(solution)/shard_map/ppermute | solution.py:14
  356.5 18.2 %collective-permute-start.2 = (bf16[16,16,512]{2,1,0:T(8,128)(2,1)S(1)}, bf16[16,16,512]{2,1,0:T(8,128)(2,1)S(1)}, u32[]{:S(2)}, u32[]{:S(2)}) collective-permute-start(bf16[16,16,512]{2,1,0:T(8,128)(2,1)S(1)} %broadcast_select_fusion.1), channel_id=1, source_target_pairs={{0,16},{4,20},{8,24},{12,28},{16,32},{20,36},{24,40},{28,44},{32,4... | collective-permute-start | bytes 786440 | tf_op jit(solution)/shard_map/ppermute | solution.py:14
  374.8 12.3 %collective-permute-start.3 = (bf16[16,16,512]{2,1,0:T(8,128)(2,1)S(1)}, bf16[16,16,512]{2,1,0:T(8,128)(2,1)S(1)}, u32[]{:S(2)}, u32[]{:S(2)}) collective-permute-start(bf16[16,16,512]{2,1,0:T(8,128)(2,1)S(1)} %broadcast_select_fusion.2), channel_id=1, source_target_pairs={{0,32},{4,36},{8,40},{12,44},{16,48},{20,52},{24,56},{28,60},{32,6... | collective-permute-start | bytes 786440 | tf_op jit(solution)/shard_map/ppermute | solution.py:14
Sparse Core Ops, SparseCore 0:
  12.4 172.2 all-gather.2
  189.0 133.5 all-gather.4
  327.2 23.1 reduce-scatter.1
